TPU v7x, 256 devices: a whole 4x4x8 slice. The times are simulated.
256 devices in a mesh: region: 32 (over z, x), shard: 8 (over y, core).
Axes of the slice: x: 4, y: 4, z: 8, core: 2. Of those that a mesh axis runs over, the one named last changes fastest.
Arguments:
- grid_rows: bfloat16 [262144, 1024], P(('region', 'shard')), may hold values from -6 to 6
- node_inputs: bfloat16 [65536, 1024], P(('region', 'shard')), may hold values from -6 to 6
- row_weight: bfloat16 [1024, 512], replicated, may hold values from -0.1875 to 0.1875
- node_weight: bfloat16 [1024, 512], replicated, may hold values from -0.1875 to 0.1875
- edge_bias: float32 [512], replicated, may hold values from -3 to 3
- edge_out_weight: bfloat16 [512, 1024], replicated, may hold values from -0.125 to 0.125
- norm_gain: float32 [1024], replicated, may hold values from 0.5 to 1.5
- attn_weight: bfloat16 [1024, 3072], replicated
- attn_out_weight: bfloat16 [1024, 1024], replicated, may hold values from -0.1875 to 0.1875
- edge_source: int32 [4096, 128], P(('region', 'shard')), may hold values from 0 to 1023
- edge_target: int32 [4096, 128], P(('region', 'shard')), may hold values from 0 to 255
- block_count: int32 [256], P(('region', 'shard')), may hold values from 1 to 16, as said below
Outputs:
- mixed: bfloat16 [65536, 1024], P(('region', 'shard'))
Inputs may be any that keep to these rules, and one draw needn't show every extreme that they name: `block_count`: some tile uses all 16 blocks. `edge_source`: blocks at or after a tile's block_count are never read.
All inputs are finite; a program needn't handle non-finite values.
Results may differ from a plain program's by a relative error of at most 0.0061.
Values may be sent and summed in bfloat16 or wider, within the bound.
A program may use at most 64 MiB of HBM per device.

v0:
```python
import jax
import jax.numpy as jnp
from jax import lax
from jax.sharding import PartitionSpec as P

HEADS = 16
WINDOW = 1120


def from_behind(value, axis, steps):
    count = lax.axis_size(axis)
    leading, last = (max(0, -steps), min(count, count - steps))
    return lax.ppermute(value, axis, [(source, source + steps) for source in range(leading, last)])


def local(
    grid_rows,
    node_inputs,
    row_weight,
    node_weight,
    edge_bias,
    edge_out_weight,
    norm_gain,
    attn_weight,
    attn_out_weight,
    edge_source,
    edge_target,
    block_count,
):
    moved = lax.all_to_all(grid_rows, "region", split_axis=0, concat_axis=0, tiled=True)
    arrived = jnp.dot(moved, row_weight, preferred_element_type=jnp.float32).astype(jnp.bfloat16)
    tile_rows = node_inputs.shape[0]
    width = node_inputs.shape[1]
    node_terms = (
        jnp.dot(node_inputs, node_weight, preferred_element_type=jnp.float32) + edge_bias
    ).astype(jnp.bfloat16)
    columns = jnp.arange(tile_rows, dtype=jnp.int32)
    used_blocks = block_count[0]

    def add_block(index, running, active):
        sources = edge_source[index]
        target = edge_target[index]
        onehot = ((target[:, None] == columns[None, :]) & active).astype(jnp.bfloat16)
        picked = jnp.take(arrived, sources, axis=0).astype(jnp.float32)
        preact = picked + jnp.dot(onehot, node_terms, preferred_element_type=jnp.float32)
        hidden = jax.nn.silu(preact).astype(jnp.bfloat16)
        message = jnp.dot(hidden, edge_out_weight, preferred_element_type=jnp.float32).astype(
            jnp.bfloat16
        )
        return running + lax.dot_general(
            onehot, message, (((0,), (0,)), ((), ())), preferred_element_type=jnp.float32
        )

    def padded_step(index, running):
        return add_block(index, running, index < used_blocks)

    start_state = node_inputs.astype(jnp.float32)
    summed = lax.fori_loop(0, edge_source.shape[0], padded_step, start_state)
    node_state = summed.astype(jnp.bfloat16)
    values_in = node_state.astype(jnp.float32)
    average = jnp.mean(values_in, axis=1, keepdims=True)
    centred = values_in - average
    spread = jnp.mean(centred * centred, axis=1, keepdims=True)
    normed = (centred * lax.rsqrt(spread + 1e-05) * norm_gain).astype(jnp.bfloat16)
    projections = jnp.dot(normed, attn_weight, preferred_element_type=jnp.float32).astype(
        jnp.bfloat16
    )
    shards = lax.axis_size("shard")
    group_width = width // shards
    heads_in = lax.all_to_all(
        projections.reshape(tile_rows, 3, shards, group_width),
        "shard",
        split_axis=2,
        concat_axis=0,
        tiled=True,
    )
    region_rows = tile_rows * shards
    queries = heads_in[:, 0, 0, :]
    keys_vals = jnp.concatenate([heads_in[:, 1, 0, :], heads_in[:, 2, 0, :]], axis=1)
    half_win = WINDOW // 2
    spans = -(-half_win // region_rows)
    earlier = [from_behind(keys_vals, "region", 1)]
    later = [from_behind(keys_vals, "region", -1)]
    joined = jnp.concatenate(earlier[::-1] + [keys_vals] + later, axis=0)
    extended = joined[spans * region_rows - half_win : spans * region_rows + region_rows + half_win]
    head_size = width // HEADS
    per_group = group_width // head_size
    scale = 1.0 / head_size**0.5
    query_heads = queries.reshape(region_rows, per_group, head_size)
    key_heads = extended[:, :group_width].reshape(region_rows + 2 * half_win, per_group, head_size)
    value_heads = extended[:, group_width:].reshape(
        region_rows + 2 * half_win, per_group, head_size
    )
    region_start = lax.axis_index("region") * region_rows
    nodes_all = region_rows * lax.axis_size("region")
    query_block = min(512, region_rows)

    def attend(block_index):
        offset = block_index * query_block
        query_part = lax.dynamic_slice_in_dim(query_heads, offset, query_block, 0)
        key_part = lax.dynamic_slice_in_dim(key_heads, offset, query_block + 2 * half_win, 0)
        value_part = lax.dynamic_slice_in_dim(value_heads, offset, query_block + 2 * half_win, 0)
        scores = (
            jnp.einsum("qhd,khd->hqk", query_part, key_part, preferred_element_type=jnp.float32)
            * scale
        )
        row_pos = jnp.arange(query_block, dtype=jnp.int32)[:, None]
        col_pos = jnp.arange(query_block + 2 * half_win, dtype=jnp.int32)[None, :]
        key_pos = region_start + offset - half_win + col_pos
        allowed = (
            (col_pos >= row_pos)
            & (col_pos < row_pos + 2 * half_win)
            & (key_pos >= 0)
            & (key_pos < nodes_all)
        )
        scores = jnp.where(allowed[None], scores, -1e30)
        largest = jnp.max(scores, axis=2, keepdims=True)
        raised = jnp.exp(scores - largest)
        weights = (raised / jnp.sum(raised, axis=2, keepdims=True)).astype(jnp.bfloat16)
        result = jnp.einsum("hqk,khd->qhd", weights, value_part, preferred_element_type=jnp.float32)
        return result.astype(jnp.bfloat16).reshape(query_block, group_width)

    attended = lax.map(attend, jnp.arange(region_rows // query_block, dtype=jnp.int32)).reshape(
        region_rows, group_width
    )
    returned = lax.all_to_all(
        attended.reshape(region_rows, 1, group_width),
        "shard",
        split_axis=0,
        concat_axis=1,
        tiled=True,
    ).reshape(tile_rows, width)
    mixed = (
        values_in + jnp.dot(returned, attn_out_weight, preferred_element_type=jnp.float32)
    ).astype(jnp.bfloat16)
    return mixed


def solution(mesh):
    placed = (
        P(("region", "shard"), None),
        P(("region", "shard"), None),
        P(),
        P(),
        P(),
        P(),
        P(),
        P(),
        P(),
        P(("region", "shard"), None),
        P(("region", "shard"), None),
        P(("region", "shard")),
    )
    return jax.shard_map(
        local, mesh=mesh, in_specs=placed, out_specs=P(("region", "shard"), None), check_vma=False
    )
```

profile of v0, /device:TPU:32, one launch (start us, length us, event | category | flops | bytes accessed | tf_op | source)
XLA Modules:
  0.0 336.9 jit_solution(10153368292534108567)
XLA Ops:
  0.0 11.4 %all-to-all-start = ((bf16[32,32,1024]{2,1,0:T(8,128)(2,1)}), bf16[32,32,1024]{2,1,0:T(8,128)(2,1)}, u32[]{:S(2)}, u32[]{:S(2)}) async-start(bf16[32,32,1024]{2,1,0:T(8,128)(2,1)} %bitcast.72), calls=%async_computation | async-start | bytes 4194304 | tf_op jit(solution)/shard_map/all_to_all | solution.py:30
  12.6 2.5 fusion.58
  15.1 46.0 %all-to-all-done = bf16[32,32,1024]{2,1,0:T(8,128)(2,1)} async-done(((bf16[32,32,1024]{2,1,0:T(8,128)(2,1)}), bf16[32,32,1024]{2,1,0:T(8,128)(2,1)}, u32[]{:S(2)}, u32[]{:S(2)}) %all-to-all-start) | async-done | bytes 2097184 | tf_op jit(solution)/shard_map/all_to_all | solution.py:30
  61.1 4.1 %convolution_convert_fusion.2 = bf16[1024,512]{1,0:T(8,128)(2,1)} fusion(bf16[1024,1024]{1,0:T(8,128)(2,1)} %bitcast.5, bf16[1024,512]{1,0:T(8,128)(2,1)} %param.18), kind=kOutput, calls=%fused_computation.60 | convolution fusion | flops 1074266112 | bytes 4194304 | tf_op jit(solution)/shard_map/dot_general | solution.py:31
  65.2 129.2 %while.27 = (s32[]{:T(128)}, f32[256,1024]{1,0:T(8,128)S(1)}, s32[16,128]{1,0:T(8,128)}, s32[]{:T(128)}, s32[16,128]{1,0:T(8,128)}, /*index=5*/bf16[1024,512]{1,...) while((s32[]{:T(128)}, f32[256,1024]{1,0:T(8,128)S(1)}, ...), condition=%wide.region_1.0_spmd.clone, body=%wide.region_0.1_spmd.clone.sunk | while | flops 235931776 | bytes 4072308 | solution.py:58
  74.0 2.2 gather_fusion
  82.0 2.2 gather_fusion
  90.1 2.2 gather_fusion
  106.3 2.2 gather_fusion
  114.3 2.2 gather_fusion
  122.4 2.2 gather_fusion
  130.5 2.2 gather_fusion
  146.6 2.2 gather_fusion
  162.8 2.2 gather_fusion
  170.9 2.2 gather_fusion
  195.1 4.7 %fusion.54 = bf16[32,8,24,128]{3,1,2,0:T(8,128)(2,1)S(1)} fusion(bf16[1024,3072]{1,0:T(8,128)(2,1)} %param.23, bf16[256,1024]{1,0:T(8,128)(2,1)S(1)} %get-tuple-element.306, f32[1024]{0:T(1024)S(1)} %copy-done.4, f32[256]{0:T(256)S(1)} %add_rsqrt_fusion, f32[256]{0:T(256)S(1)} %broadcast_multiply_fusion), kind=kOutput, calls=%fused_computation.59 | convolution fusion | flops 1612709888 | bytes 8394752 | tf_op jit(solution)/shard_map/dot_general | solution.py:65
  200.5 25.9 %all_to_all.45 = bf16[256,3,8,128]{3,0,1,2:T(8,128)(2,1)S(1)} all-to-all(bf16[256,3,8,128]{3,0,1,2:T(8,128)(2,1)S(1)} %copy.27), channel_id=1, replica_groups=mesh['region'=32,'shard'=8] {'shard'}, dimensions={2} | all-to-all | bytes 3145728 | tf_op jit(solution)/shard_map/all_to_all | solution.py:70
  228.5 3.4 collective-permute-start
  231.8 4.8 %collective-permute-start.1 = (bf16[2048,256]{1,0:T(8,128)(2,1)}, bf16[2048,256]{1,0:T(8,128)(2,1)}, u32[]{:S(2)}, u32[]{:S(2)}) collective-permute-start(bf16[2048,256]{1,0:T(8,128)(2,1)} %pad_maximum_fusion), channel_id=1, source_target_pairs={{8,0},{16,8},{24,16},{32,24},{40,32},{48,40},{56,48},{64,56},{72,6... | collective-permute-start | bytes 3145736 | tf_op jit(solution)/shard_map/ppermute | solution.py:13
  238.7 18.6 %collective-permute-done = bf16[2048,256]{1,0:T(8,128)(2,1)} collective-permute-done((bf16[2048,256]{1,0:T(8,128)(2,1)}, bf16[2048,256]{1,0:T(8,128)(2,1)}, u32[]{:S(2)}, u32[]{:S(2)}) %collective-permute-start) | collective-permute-done | bytes 1048608 | tf_op jit(solution)/shard_map/ppermute | solution.py:13
  258.5 2.4 pad_maximum_fusion.1
  260.9 2.3 copy.30
  264.9 47.9 %while.26 = (s32[]{:T(128)}, bf16[4,512,128]{2,1,0:T(8,128)(2,1)}, s32[4]{0:T(128)S(1)}, bf16[3168,2,64]{0,2,1:T(8,128)(2,1)}, s32[]{:T(128)}, /*index=5*/bf16[2...) while((s32[]{:T(128)}, bf16[4,512,128]{2,1,0:T(8,128)(2,1)}, ...), condition=%wide.region_7.8_spmd, body=%wide.region_4.7_spmd.sunk | while | flops 661022208 | bytes 4723316 | solution.py:123
  267.5 3.8 %fusion.104 = f32[2,512]{1,0:T(2,128)S(1)} fusion(pred[512,1632]{0,1:T(8,128)(4,1)S(1)} %fusion.103, bf16[3168,2,64]{0,2,1:T(8,128)(2,1)} %get-tuple-element.468, s32[]{:T(128)S(6)} %select_n.85, bf16[2048,2,64]{0,2,1:T(8,128)(2,1)} %get-tuple-element.467, s32[]{:T(128)S(6)} %select_n.86), kind=kOutput, calls=%fused_computation.81.clone.1 | convolution fusion | flops 220595808 | bytes 1396744 | tf_op jit(solution)/shard_map/while/body/eval_jaxpr/sub | solution.py:118
  271.3 4.8 %fusion.105 = bf16[2,64,512]{2,1,0:T(8,128)(2,1)S(1)} fusion(f32[2,512]{1,0:T(2,128)S(1)} %fusion.104, bf16[3168,2,64]{0,2,1:T(8,128)(2,1)} %get-tuple-element.465, s32[]{:T(128)S(6)} %select_n.85, pred[512,1632]{0,1:T(8,128)(4,1)S(1)} %fusion.103, bf16[3168,2,64]{0,2,1:T(8,128)(2,1)} %get-tuple-element.468, ...), kind=kOutput, calls=%fused_computation.16.clone.1 | convolution fusion | flops 436243040 | bytes 1955328 | tf_op jit(solution)/shard_map/while/body/eval_jaxpr/hqk,khd->qhd/dot_general | solution.py:120
  279.4 3.8 %fusion.104 = f32[2,512]{1,0:T(2,128)S(1)} fusion(pred[512,1632]{0,1:T(8,128)(4,1)S(1)} %fusion.103, bf16[3168,2,64]{0,2,1:T(8,128)(2,1)} %get-tuple-element.468, s32[]{:T(128)S(6)} %select_n.85, bf16[2048,2,64]{0,2,1:T(8,128)(2,1)} %get-tuple-element.467, s32[]{:T(128)S(6)} %select_n.86), kind=kOutput, calls=%fused_computation.81.clone.1 | convolution fusion | flops 220595808 | bytes 1396744 | tf_op jit(solution)/shard_map/while/body/eval_jaxpr/sub | solution.py:118
  283.2 4.8 %fusion.105 = bf16[2,64,512]{2,1,0:T(8,128)(2,1)S(1)} fusion(f32[2,512]{1,0:T(2,128)S(1)} %fusion.104, bf16[3168,2,64]{0,2,1:T(8,128)(2,1)} %get-tuple-element.465, s32[]{:T(128)S(6)} %select_n.85, pred[512,1632]{0,1:T(8,128)(4,1)S(1)} %fusion.103, bf16[3168,2,64]{0,2,1:T(8,128)(2,1)} %get-tuple-element.468, ...), kind=kOutput, calls=%fused_computation.16.clone.1 | convolution fusion | flops 436243040 | bytes 1955328 | tf_op jit(solution)/shard_map/while/body/eval_jaxpr/hqk,khd->qhd/dot_general | solution.py:120
  291.4 3.8 %fusion.104 = f32[2,512]{1,0:T(2,128)S(1)} fusion(pred[512,1632]{0,1:T(8,128)(4,1)S(1)} %fusion.103, bf16[3168,2,64]{0,2,1:T(8,128)(2,1)} %get-tuple-element.468, s32[]{:T(128)S(6)} %select_n.85, bf16[2048,2,64]{0,2,1:T(8,128)(2,1)} %get-tuple-element.467, s32[]{:T(128)S(6)} %select_n.86), kind=kOutput, calls=%fused_computation.81.clone.1 | convolution fusion | flops 220595808 | bytes 1396744 | tf_op jit(solution)/shard_map/while/body/eval_jaxpr/sub | solution.py:118
  295.2 4.8 %fusion.105 = bf16[2,64,512]{2,1,0:T(8,128)(2,1)S(1)} fusion(f32[2,512]{1,0:T(2,128)S(1)} %fusion.104, bf16[3168,2,64]{0,2,1:T(8,128)(2,1)} %get-tuple-element.465, s32[]{:T(128)S(6)} %select_n.85, pred[512,1632]{0,1:T(8,128)(4,1)S(1)} %fusion.103, bf16[3168,2,64]{0,2,1:T(8,128)(2,1)} %get-tuple-element.468, ...), kind=kOutput, calls=%fused_computation.16.clone.1 | convolution fusion | flops 436243040 | bytes 1955328 | tf_op jit(solution)/shard_map/while/body/eval_jaxpr/hqk,khd->qhd/dot_general | solution.py:120
  303.4 3.8 %fusion.104 = f32[2,512]{1,0:T(2,128)S(1)} fusion(pred[512,1632]{0,1:T(8,128)(4,1)S(1)} %fusion.103, bf16[3168,2,64]{0,2,1:T(8,128)(2,1)} %get-tuple-element.468, s32[]{:T(128)S(6)} %select_n.85, bf16[2048,2,64]{0,2,1:T(8,128)(2,1)} %get-tuple-element.467, s32[]{:T(128)S(6)} %select_n.86), kind=kOutput, calls=%fused_computation.81.clone.1 | convolution fusion | flops 220595808 | bytes 1396744 | tf_op jit(solution)/shard_map/while/body/eval_jaxpr/sub | solution.py:118
  307.2 4.8 %fusion.105 = bf16[2,64,512]{2,1,0:T(8,128)(2,1)S(1)} fusion(f32[2,512]{1,0:T(2,128)S(1)} %fusion.104, bf16[3168,2,64]{0,2,1:T(8,128)(2,1)} %get-tuple-element.465, s32[]{:T(128)S(6)} %select_n.85, pred[512,1632]{0,1:T(8,128)(4,1)S(1)} %fusion.103, bf16[3168,2,64]{0,2,1:T(8,128)(2,1)} %get-tuple-element.468, ...), kind=kOutput, calls=%fused_computation.16.clone.1 | convolution fusion | flops 436243040 | bytes 1955328 | tf_op jit(solution)/shard_map/while/body/eval_jaxpr/hqk,khd->qhd/dot_general | solution.py:120
  316.5 13.8 %all_to_all.46 = bf16[8,2,16384]{2,1,0:T(2,128)(2,1)S(1)} all-to-all(bf16[8,2,16384]{2,1,0:T(2,128)(2,1)} %reshape.170), channel_id=1, replica_groups=mesh['region'=32,'shard'=8] {'shard'}, dimensions={0} | all-to-all | bytes 1048576 | tf_op jit(solution)/shard_map/all_to_all | solution.py:126
  (161 shorter events, 126.7 us)
Async XLA Ops:
  0.0 335.3 %copy-start = (bf16[1024,1024]{1,0:T(8,128)(2,1)S(1)}, bf16[1024,1024]{1,0:T(8,128)(2,1)}, u32[]{:S(2)}) copy-start(bf16[1024,1024]{1,0:T(8,128)(2,1)} %param.24) | copy-start | bytes 6291460
  0.0 12.5 %copy-start.5 = (f32[512]{0:T(512)S(1)}, f32[512]{0:T(512)}, u32[]{:S(2)}) copy-start(f32[512]{0:T(512)} %param.20) | copy-start | bytes 6148
  0.0 61.1 %all-to-all-start = ((bf16[32,32,1024]{2,1,0:T(8,128)(2,1)}), bf16[32,32,1024]{2,1,0:T(8,128)(2,1)}, u32[]{:S(2)}, u32[]{:S(2)}) async-start(bf16[32,32,1024]{2,1,0:T(8,128)(2,1)} %bitcast.72), calls=%async_computation | async-start | bytes 4194304 | tf_op jit(solution)/shard_map/all_to_all | solution.py:30
  194.4 0.7 copy-start.4
  194.5 5.3 %copy-start.1 = (bf16[256,1024]{1,0:T(8,128)(2,1)}, bf16[256,1024]{1,0:T(8,128)(2,1)S(1)}, u32[]{:S(2)}) copy-start(bf16[256,1024]{1,0:T(8,128)(2,1)S(1)} %get-tuple-element.306) | copy-start | bytes 1572868
  228.5 28.8 %collective-permute-start = (bf16[2048,256]{1,0:T(8,128)(2,1)}, bf16[2048,256]{1,0:T(8,128)(2,1)}, u32[]{:S(2)}, u32[]{:S(2)}) collective-permute-start(bf16[2048,256]{1,0:T(8,128)(2,1)} %pad_maximum_fusion), channel_id=1, source_target_pairs={{0,8},{8,16},{16,24},{24,32},{32,40},{40,48},{48,56},{56,64},{64,7... | collective-permute-start | bytes 3145736 | tf_op jit(solution)/shard_map/ppermute | solution.py:13
  231.8 26.7 %collective-permute-start.1 = (bf16[2048,256]{1,0:T(8,128)(2,1)}, bf16[2048,256]{1,0:T(8,128)(2,1)}, u32[]{:S(2)}, u32[]{:S(2)}) collective-permute-start(bf16[2048,256]{1,0:T(8,128)(2,1)} %pad_maximum_fusion), channel_id=1, source_target_pairs={{8,0},{16,8},{24,16},{32,24},{40,32},{48,40},{56,48},{64,56},{72,6... | collective-permute-start | bytes 3145736 | tf_op jit(solution)/shard_map/ppermute | solution.py:13
  260.9 2.3 copy-start.3
  330.2 5.1 %copy-start.2 = (bf16[256,1024]{1,0:T(8,128)(2,1)S(1)}, bf16[256,1024]{1,0:T(8,128)(2,1)}, u32[]{:S(2)}) copy-start(bf16[256,1024]{1,0:T(8,128)(2,1)} %copy-done.1) | copy-start | bytes 1572868
where the time goes:
time: 344 us; the launch traced here: 337 us
  matrix products  96.2 us (28%)
  local copies, waits for them, and re-layouts  66.8 us (19%)
  waiting for transfers between devices  65.8 us (19%)
  blocking collectives  39.6 us (12%)
  other arithmetic  35.3 us (10%)
  starting transfers between devices  19.5 us (6%)
  loops' own time  13.4 us (4%)
    all_to_all x1, waiting for transfers between devices, local(): lax.all_to_all(grid_rows, 'region', split_axis=0, concat_axis=0, tiled=True)  46 us
    gather x16, local copies, waits for them, and re-layouts, add_block(): picked = jnp.take(arrived, sources, axis=0).astype(jnp.float32)  35.7 us
    dot_general x16, matrix products, add_block(): lax.dot_general(onehot, message, (((0,), (0,)), ((), ())), preferred_elem...  29.3 us
    all_to_all x1, blocking collectives, local(): lax.all_to_all(projections.reshape(tile_rows, 3, shards, group_width), 's...  25.9 us
    ppermute x2, waiting for transfers between devices, from_behind(): lax.ppermute(value, axis, [(source, source + steps) for source in range(l...  19.8 us
    dot_general x16, matrix products, add_block(): jnp.dot(onehot, node_terms, preferred_element_type=jnp.float32)  19.6 us
    dot_general x4, matrix products, attend(): jnp.einsum('hqk,khd->qhd', weights, value_part, preferred_element_type=jn...  19.3 us
    sub x4, matrix products, attend(): raised = jnp.exp(scores - largest)  15.2 us
  transfers between devices with their start and end apart: 3, of which 3 were waited for; matrix products, arithmetic and copies ran while one was open for 2% of the time, Pallas kernels for 0%

commit v1 on v0

v1 whole, which is shorter than its diff:
```python
import jax
import jax.numpy as jnp
from jax import lax
from jax.experimental import pallas as pl
from jax.experimental.pallas import tpu as pltpu
from jax.sharding import PartitionSpec as P

HALF = 560
KEYS = 1408
CHUNKS = (
    (560, 256, 0),
    (304, 256, -1),
    (816, 256, 1),
    (48, 256, -2),
    (1072, 256, 2),
    (0, 48, -3),
    (1328, 80, 3),
)
LOG2E = 1.4426950408889634
F32 = jnp.float32
BF16 = jnp.bfloat16


def edge_kernel(count_ref, arrived, nodes, node_weight, bias, source, target, out, table, hidden, picks):
    blocks, width = source.shape
    rows = arrived.shape[0]
    tile = nodes.shape[0]
    used = count_ref[0]
    table[pl.ds(0, rows), :] = arrived[...]
    table[pl.ds(rows, tile), :] = (
        jnp.dot(nodes[...], node_weight[...], preferred_element_type=F32) + bias[...]
    ).astype(BF16)
    source_cols = jnp.transpose(source[...])
    target_cols = jnp.transpose(target[...])
    lane_rows = lax.broadcasted_iota(jnp.int32, (width, rows), 1)
    lane_tile = lax.broadcasted_iota(jnp.int32, (width, tile), 1)
    sub_tile = lax.broadcasted_iota(jnp.int32, (tile, width), 0)
    for block in range(blocks):
        span = pl.ds(block * width, width)
        onehot = jnp.concatenate(
            [
                (source_cols[:, block : block + 1] == lane_rows).astype(F32).astype(BF16),
                (target_cols[:, block : block + 1] == lane_tile).astype(F32).astype(BF16),
            ],
            axis=1,
        )
        pre = jnp.dot(onehot, table[...], preferred_element_type=F32)
        hidden[span, :] = (0.5 * pre * (1.0 + jnp.tanh(0.5 * pre))).astype(BF16)
        goal = jnp.where(block < used, target[block : block + 1, :], -1)
        picks[:, span] = (goal == sub_tile).astype(F32).astype(BF16)
    out[...] = jnp.dot(picks[...], hidden[...], preferred_element_type=F32).astype(BF16)


def window_kernel(sums, nodes, edge_out, gain, attn_weight, out_weight, mixed, queries, keys, values, attended, state):
    tile, width = mixed.shape
    own = CHUNKS[0][0]
    tiles = lax.axis_size("region") * lax.axis_size("shard")
    me = lax.axis_index("region") * lax.axis_size("shard") + lax.axis_index("shard")
    for first, rows, away in CHUNKS:
        span = pl.ds(first, rows)
        summed, embedded = sums[span, :], nodes[span, :]
        there = (me + away >= 0) & (me + away < tiles)
        if away:
            summed = jnp.where(there, summed, sums[pl.ds(own, rows), :])
            embedded = jnp.where(there, embedded, nodes[pl.ds(own, rows), :])
        held = (
            embedded.astype(F32) + jnp.dot(summed, edge_out[...], preferred_element_type=F32)
        ).astype(BF16)
        if not away:
            state[...] = held
        held = held.astype(F32)
        centred = held - jnp.mean(held, axis=1, keepdims=True)
        spread = jnp.mean(centred * centred, axis=1, keepdims=True)
        normed = (centred * lax.rsqrt(spread + 1e-05) * gain[...]).astype(BF16)
        keys[span, :] = jnp.dot(
            normed, attn_weight[:, width : 2 * width], preferred_element_type=F32
        ).astype(BF16)
        value = jnp.dot(normed, attn_weight[:, 2 * width :], preferred_element_type=F32)
        flag = there.astype(F32) if away else 1.0
        values[span, :] = (value * flag).astype(BF16)
        if not away:
            queries[...] = (
                jnp.dot(normed, attn_weight[:, :width], preferred_element_type=F32)
                * (LOG2E * 0.125)
            ).astype(BF16)
    spot = lax.broadcasted_iota(jnp.int32, (KEYS, 128), 0) - own + me * tile
    live = ((spot >= 0) & (spot < tiles * tile)).astype(F32).astype(BF16)
    lanes = lax.broadcasted_iota(jnp.int32, (tile, 128), 1)
    left_row = lax.broadcasted_iota(jnp.int32, (2 * tile, 256), 0) % tile
    left_key = lax.broadcasted_iota(jnp.int32, (2 * tile, 256), 1)
    right_row = lax.broadcasted_iota(jnp.int32, (2 * tile, KEYS - 1024), 0) % tile
    right_key = lax.broadcasted_iota(jnp.int32, (2 * tile, KEYS - 1024), 1) + 1024

    def pair(index, carry):
        span = pl.ds(pl.multiple_of(index * 128, 128), 128)
        query = queries[:, span]
        zero = jnp.zeros_like(query)
        query = jnp.concatenate(
            [jnp.where(lanes < 64, query, zero), jnp.where(lanes >= 64, query, zero)], axis=0
        )
        scores = lax.dot_general(
            query, keys[:, span], (((1,), (1,)), ((), ())), preferred_element_type=F32
        )
        scores = jnp.concatenate(
            [
                jnp.where(left_key >= left_row, scores[:, :256], -1e30),
                scores[:, 256:1024],
                jnp.where(right_key < right_row + 2 * HALF, scores[:, 1024:], -1e30),
            ],
            axis=1,
        )
        raised = jnp.exp2(scores - jnp.max(scores, axis=1, keepdims=True)).astype(BF16)
        both = jnp.dot(
            raised, jnp.concatenate([values[:, span], live], axis=1), preferred_element_type=F32
        )
        both = both[:, :128] / both[:, 128:]
        attended[:, span] = jnp.where(lanes < 64, both[:tile], both[tile:]).astype(BF16)
        return carry

    lax.fori_loop(0, width // 128, pair, 0)
    mixed[...] = (
        state[...].astype(F32)
        + jnp.dot(attended[...], out_weight[...], preferred_element_type=F32)
    ).astype(BF16)


def in_vmem(count):
    return [pl.BlockSpec(memory_space=pltpu.VMEM)] * count


def extend(own):
    tiles = lax.axis_size("region") * lax.axis_size("shard")
    pieces = {0: own}
    for _, rows, away in CHUNKS[1:]:
        part = own if rows == own.shape[0] else (own[-rows:] if away < 0 else own[:rows])
        routes = [(i, i - away) for i in range(tiles) if 0 <= i - away < tiles]
        pieces[away] = lax.ppermute(part, ("region", "shard"), routes)
    return jnp.concatenate([pieces[away] for away in sorted(pieces)], axis=0)


def local(
    grid_rows,
    node_inputs,
    row_weight,
    node_weight,
    edge_bias,
    edge_out_weight,
    norm_gain,
    attn_weight,
    attn_out_weight,
    edge_source,
    edge_target,
    block_count,
):
    tile, width = node_inputs.shape
    rows = grid_rows.shape[0]
    hidden = row_weight.shape[1]
    edges = edge_source.shape[0] * edge_source.shape[1]
    projected = jnp.dot(grid_rows, row_weight, preferred_element_type=F32).astype(BF16)
    arrived = lax.all_to_all(projected, "region", split_axis=0, concat_axis=0, tiled=True)
    all_nodes = extend(node_inputs)
    sums = pl.pallas_call(
        edge_kernel,
        out_shape=jax.ShapeDtypeStruct((tile, hidden), BF16),
        in_specs=[pl.BlockSpec(memory_space=pltpu.SMEM)] + in_vmem(6),
        out_specs=in_vmem(1)[0],
        scratch_shapes=[
            pltpu.VMEM((rows + tile, hidden), BF16),
            pltpu.VMEM((edges, hidden), BF16),
            pltpu.VMEM((tile, edges), BF16),
        ],
        name="edges",
    )(block_count, arrived, node_inputs, node_weight, edge_bias[None], edge_source, edge_target)
    all_sums = extend(sums)
    return pl.pallas_call(
        window_kernel,
        out_shape=jax.ShapeDtypeStruct((tile, width), BF16),
        in_specs=in_vmem(6),
        out_specs=in_vmem(1)[0],
        scratch_shapes=[
            pltpu.VMEM((tile, width), BF16),
            pltpu.VMEM((KEYS, width), BF16),
            pltpu.VMEM((KEYS, width), BF16),
            pltpu.VMEM((tile, width), BF16),
            pltpu.VMEM((tile, width), BF16),
        ],
        name="window",
    )(all_sums, all_nodes, edge_out_weight, norm_gain[None], attn_weight, attn_out_weight)


def solution(mesh):
    placed = (
        P(("region", "shard"), None),
        P(("region", "shard"), None),
        P(),
        P(),
        P(),
        P(),
        P(),
        P(),
        P(),
        P(("region", "shard"), None),
        P(("region", "shard"), None),
        P(("region", "shard")),
    )
    return jax.shard_map(
        local, mesh=mesh, in_specs=placed, out_specs=P(("region", "shard"), None), check_vma=False
    )
```

time: 344 us -> 146 us (0.42)
  the two profiles are of different devices: /device:TPU:32 before, /device:TPU:119 now
where the time goes in v1:
time: 146 us; the launch traced here: 145 us
  starting transfers between devices  67.8 us (46%)
  Pallas kernels  38.8 us (27%)
  waiting for transfers between devices  20.1 us (14%)
  local copies, waits for them, and re-layouts  13.9 us (10%)
  matrix products  3.44 us (2%)
    ppermute x12, starting transfers between devices, extend(): pieces[away] = lax.ppermute(part, ('region', 'shard'), routes)  58.2 us
    pallas_call x1, Pallas kernels, local(): pl.pallas_call(window_kernel, out_shape=jax.ShapeDtypeStruct((tile, width...  32.5 us
    ppermute x12, waiting for transfers between devices, extend(): pieces[away] = lax.ppermute(part, ('region', 'shard'), routes)  20.1 us
    unnamed x22, local copies, waits for them, and re-layouts  9.65 us
    all_to_all x1, starting transfers between devices, local(): lax.all_to_all(projected, 'region', split_axis=0, concat_axis=0, tiled=True)  9.65 us
    pallas_call x1, Pallas kernels, local(): pl.pallas_call(edge_kernel, out_shape=jax.ShapeDtypeStruct((tile, hidden)...  6.29 us
    dot_general x1, matrix products, local(): jnp.dot(grid_rows, row_weight, preferred_element_type=F32).astype(BF16)  3.44 us
  transfers between devices with their start and end apart: 13, of which 3 were waited for; matrix products, arithmetic and copies ran while one was open for 7% of the time, Pallas kernels for 4%

profile of v1, /device:TPU:119, one launch (start us, length us, event | category | flops | bytes accessed | tf_op | source)
XLA Modules:
  0.0 145.0 jit_solution(8559369286864807149)
XLA Ops:
  0.0 1.6 %copy-done = bf16[1024,1024]{1,0:T(8,128)(2,1)S(1)} copy-done((bf16[1024,1024]{1,0:T(8,128)(2,1)S(1)}, bf16[1024,1024]{1,0:T(8,128)(2,1)}, u32[]{:S(2)}) %copy-start) | copy-done | bytes 2097176
  1.6 3.4 %convolution_convert_fusion = bf16[1024,512]{1,0:T(8,128)(2,1)} fusion(bf16[1024,1024]{1,0:T(8,128)(2,1)S(1)} %copy-done, bf16[1024,512]{1,0:T(8,128)(2,1)} %param.14), kind=kOutput, calls=%fused_computation | convolution fusion | flops 1074266112 | bytes 4194304 | tf_op jit(solution)/shard_map/dot_general | solution.py:159
  5.0 9.6 %all-to-all-start = ((bf16[32,32,512]{2,1,0:T(8,128)(2,1)}), bf16[32,32,512]{2,1,0:T(8,128)(2,1)S(1)}, u32[]{:S(2)}, u32[]{:S(2)}) async-start(bf16[32,32,512]{2,1,0:T(8,128)(2,1)} %bitcast.7), calls=%async_computation | async-start | bytes 2097152 | tf_op jit(solution)/shard_map/all_to_all | solution.py:160
  14.7 3.0 %collective-permute-start.7 = (bf16[256,1024]{1,0:T(8,128)(2,1)}, bf16[256,1024]{1,0:T(8,128)(2,1)S(1)}, u32[]{:S(2)}, u32[]{:S(2)}) collective-permute-start(bf16[256,1024]{1,0:T(8,128)(2,1)} %nodes.1), channel_id=1, source_target_pairs={{0,2},{1,3},{2,4},{3,5},{4,6},{5,7},{6,8},{7,9},{8,10},{9,11},{10,... | collective-permute-start | bytes 1572872 | tf_op jit(solution)/shard_map/ppermute | solution.py:137
  17.8 5.4 %collective-permute-start.8 = (bf16[256,1024]{1,0:T(8,128)(2,1)}, bf16[256,1024]{1,0:T(8,128)(2,1)S(1)}, u32[]{:S(2)}, u32[]{:S(2)}) collective-permute-start(bf16[256,1024]{1,0:T(8,128)(2,1)} %nodes.1), channel_id=1, source_target_pairs={{0,1},{1,2},{2,3},{3,4},{4,5},{5,6},{6,7},{7,8},{8,9},{9,10},{10,1... | collective-permute-start | bytes 1572872 | tf_op jit(solution)/shard_map/ppermute | solution.py:137
  23.1 0.9 slice.14
  24.0 2.3 %collective-permute-start.6 = (bf16[48,1024]{1,0:T(8,128)(2,1)S(1)}, bf16[48,1024]{1,0:T(8,128)(2,1)S(1)}, u32[]{:S(2)}, u32[]{:S(2)}) collective-permute-start(bf16[48,1024]{1,0:T(8,128)(2,1)S(1)} %slice.14), channel_id=1, source_target_pairs={{0,3},{1,4},{2,5},{3,6},{4,7},{5,8},{6,9},{7,10},{8,11},{9,12},{10... | collective-permute-start | bytes 294920 | tf_op jit(solution)/shard_map/ppermute | solution.py:137
  26.3 3.2 %collective-permute-start.9 = (bf16[256,1024]{1,0:T(8,128)(2,1)}, bf16[256,1024]{1,0:T(8,128)(2,1)S(1)}, u32[]{:S(2)}, u32[]{:S(2)}) collective-permute-start(bf16[256,1024]{1,0:T(8,128)(2,1)} %nodes.1), channel_id=1, source_target_pairs={{1,0},{2,1},{3,2},{4,3},{5,4},{6,5},{7,6},{8,7},{9,8},{10,9},{11,1... | collective-permute-start | bytes 1572872 | tf_op jit(solution)/shard_map/ppermute | solution.py:137
  29.5 2.1 %collective-permute-start.10 = (bf16[256,1024]{1,0:T(8,128)(2,1)}, bf16[256,1024]{1,0:T(8,128)(2,1)}, u32[]{:S(2)}, u32[]{:S(2)}) collective-permute-start(bf16[256,1024]{1,0:T(8,128)(2,1)} %nodes.1), channel_id=1, source_target_pairs={{2,0},{3,1},{4,2},{5,3},{6,4},{7,5},{8,6},{9,7},{10,8},{11,9},{12,... | collective-permute-start | bytes 1572872 | tf_op jit(solution)/shard_map/ppermute | solution.py:137
  31.6 0.9 slice.15
  33.2 5.6 %collective-permute-done.6 = bf16[48,1024]{1,0:T(8,128)(2,1)S(1)} collective-permute-done((bf16[48,1024]{1,0:T(8,128)(2,1)S(1)}, bf16[48,1024]{1,0:T(8,128)(2,1)S(1)}, u32[]{:S(2)}, u32[]{:S(2)}) %collective-permute-start.6) | collective-permute-done | bytes 98336 | tf_op jit(solution)/shard_map/ppermute | solution.py:137
  38.8 13.1 %collective-permute-start.11 = (bf16[80,1024]{1,0:T(8,128)(2,1)S(1)}, bf16[80,1024]{1,0:T(8,128)(2,1)S(1)}, u32[]{:S(2)}, u32[]{:S(2)}) collective-permute-start(bf16[80,1024]{1,0:T(8,128)(2,1)S(1)} %slice.15), channel_id=1, source_target_pairs={{3,0},{4,1},{5,2},{6,3},{7,4},{8,5},{9,6},{10,7},{11,8},{12,9},{13... | collective-permute-start | bytes 491528 | tf_op jit(solution)/shard_map/ppermute | solution.py:137
  52.6 0.8 constant_dynamic-update-slice_fusion.12
  53.4 0.8 constant_dynamic-update-slice_fusion.11
  54.3 0.8 constant_dynamic-update-slice_fusion.10
  55.1 0.8 constant_dynamic-update-slice_fusion.9
  56.0 1.0 copy-done.1
  56.9 6.3 %edges.1 = bf16[256,512]{1,0:T(8,128)(2,1)} custom-call(s32[1]{0:T(128)S(6)} %copy.25.count_ref, bf16[1024,512]{1,0:T(8,128)(2,1)} %bitcast.6, bf16[256,1024]{1,0:T(8,128)(2,1)} %nodes.1, bf16[1024,512]{1,0:T(8,128)(2,1)} %node_weight.1, f32[1,512]{1,0:T(1,128)} %bitcast.9, s32[16,128]{1,0:T(8,128)} %source.1, s32[16,128]{1,0:T(8,128)} %target.1), custom_call_target="tpu_custom_call" | custom-call | tf_op jit(solution)/shard_map/edges/pallas_call | solution.py:162
  63.2 10.1 %collective-permute-start.1 = (bf16[256,512]{1,0:T(8,128)(2,1)}, bf16[256,512]{1,0:T(8,128)(2,1)S(1)}, u32[]{:S(2)}, u32[]{:S(2)}) collective-permute-start(bf16[256,512]{1,0:T(8,128)(2,1)} %edges.1), channel_id=1, source_target_pairs={{0,2},{1,3},{2,4},{3,5},{4,6},{5,7},{6,8},{7,9},{8,10},{9,11},{10,... | collective-permute-start | bytes 786440 | tf_op jit(solution)/shard_map/ppermute | solution.py:137
  73.4 1.9 %constant_dynamic-update-slice_fusion.8 = bf16[1408,1024]{1,0:T(8,128)(2,1)} fusion(bf16[1408,1024]{1,0:T(8,128)(2,1)} %constant_dynamic-update-slice_fusion.9, bf16[256,1024]{1,0:T(8,128)(2,1)} %collective-permute-done.10), kind=kLoop, calls=%fused_computation.9 | loop fusion | bytes 1048576
  75.2 0.8 slice.16
  76.0 5.7 %collective-permute-start.2 = (bf16[256,512]{1,0:T(8,128)(2,1)}, bf16[256,512]{1,0:T(8,128)(2,1)S(1)}, u32[]{:S(2)}, u32[]{:S(2)}) collective-permute-start(bf16[256,512]{1,0:T(8,128)(2,1)} %edges.1), channel_id=1, source_target_pairs={{0,1},{1,2},{2,3},{3,4},{4,5},{5,6},{6,7},{7,8},{8,9},{9,10},{10,1... | collective-permute-start | bytes 786440 | tf_op jit(solution)/shard_map/ppermute | solution.py:137
  81.8 6.0 %collective-permute-start = (bf16[48,512]{1,0:T(8,128)(2,1)S(1)}, bf16[48,512]{1,0:T(8,128)(2,1)S(1)}, u32[]{:S(2)}, u32[]{:S(2)}) collective-permute-start(bf16[48,512]{1,0:T(8,128)(2,1)S(1)} %slice.16), channel_id=1, source_target_pairs={{0,3},{1,4},{2,5},{3,6},{4,7},{5,8},{6,9},{7,10},{8,11},{9,12},{10... | collective-permute-start | bytes 147464 | tf_op jit(solution)/shard_map/ppermute | solution.py:137
  87.8 0.7 constant_dynamic-update-slice_fusion.7.nodes
  88.5 3.2 %collective-permute-start.3 = (bf16[256,512]{1,0:T(8,128)(2,1)}, bf16[256,512]{1,0:T(8,128)(2,1)S(1)}, u32[]{:S(2)}, u32[]{:S(2)}) collective-permute-start(bf16[256,512]{1,0:T(8,128)(2,1)} %edges.1), channel_id=1, source_target_pairs={{1,0},{2,1},{3,2},{4,3},{5,4},{6,5},{7,6},{8,7},{9,8},{10,9},{11,1... | collective-permute-start | bytes 786440 | tf_op jit(solution)/shard_map/ppermute | solution.py:137
  91.7 1.9 %collective-permute-start.4 = (bf16[256,512]{1,0:T(8,128)(2,1)}, bf16[256,512]{1,0:T(8,128)(2,1)S(1)}, u32[]{:S(2)}, u32[]{:S(2)}) collective-permute-start(bf16[256,512]{1,0:T(8,128)(2,1)} %edges.1), channel_id=1, source_target_pairs={{2,0},{3,1},{4,2},{5,3},{6,4},{7,5},{8,6},{9,7},{10,8},{11,9},{12,... | collective-permute-start | bytes 786440 | tf_op jit(solution)/shard_map/ppermute | solution.py:137
  93.6 0.9 slice.17
  94.5 2.1 %collective-permute-start.5 = (bf16[80,512]{1,0:T(8,128)(2,1)S(1)}, bf16[80,512]{1,0:T(8,128)(2,1)S(1)}, u32[]{:S(2)}, u32[]{:S(2)}) collective-permute-start(bf16[80,512]{1,0:T(8,128)(2,1)S(1)} %slice.17), channel_id=1, source_target_pairs={{3,0},{4,1},{5,2},{6,3},{7,4},{8,5},{9,6},{10,7},{11,8},{12,9},{13... | collective-permute-start | bytes 245768 | tf_op jit(solution)/shard_map/ppermute | solution.py:137
  96.8 5.2 %collective-permute-done.4 = bf16[256,512]{1,0:T(8,128)(2,1)S(1)} collective-permute-done((bf16[256,512]{1,0:T(8,128)(2,1)}, bf16[256,512]{1,0:T(8,128)(2,1)S(1)}, u32[]{:S(2)}, u32[]{:S(2)}) %collective-permute-start.4) | collective-permute-done | bytes 262176 | tf_op jit(solution)/shard_map/ppermute | solution.py:137
  102.1 9.2 %collective-permute-done.5 = bf16[80,512]{1,0:T(8,128)(2,1)S(1)} collective-permute-done((bf16[80,512]{1,0:T(8,128)(2,1)S(1)}, bf16[80,512]{1,0:T(8,128)(2,1)S(1)}, u32[]{:S(2)}, u32[]{:S(2)}) %collective-permute-start.5) | collective-permute-done | bytes 81952 | tf_op jit(solution)/shard_map/ppermute | solution.py:137
  111.3 1.1 copy-done.4
  112.4 32.5 %window.1 = bf16[256,1024]{1,0:T(8,128)(2,1)} custom-call(bf16[1408,512]{1,0:T(8,128)(2,1)} %copy-done.4, bf16[1408,1024]{1,0:T(8,128)(2,1)} %constant_dynamic-update-slice_fusion.7.nodes, bf16[512,1024]{1,0:T(8,128)(2,1)} %edge_out.1, f32[1,1024]{1,0:T(1,128)} %bitcast.8, bf16[1024,3072]{1,0:T(8,128)(2,1)} %attn_weight.1, bf16[1024,1024]{1,0:T(8,128)(2,1)} %out_weight.1), custom_call_target="tpu_custom_call" | custom-call | tf_op jit(solution)/shard_map/window/pallas_call | solution.py:175
  (25 shorter events, 0.8 us)
Async XLA Ops:
  0.0 1.6 %copy-start = (bf16[1024,1024]{1,0:T(8,128)(2,1)S(1)}, bf16[1024,1024]{1,0:T(8,128)(2,1)}, u32[]{:S(2)}) copy-start(bf16[1024,1024]{1,0:T(8,128)(2,1)} %param.12) | copy-start | bytes 6291460
  5.0 50.9 %all-to-all-start = ((bf16[32,32,512]{2,1,0:T(8,128)(2,1)}), bf16[32,32,512]{2,1,0:T(8,128)(2,1)S(1)}, u32[]{:S(2)}, u32[]{:S(2)}) async-start(bf16[32,32,512]{2,1,0:T(8,128)(2,1)} %bitcast.7), calls=%async_computation | async-start | bytes 2097152 | tf_op jit(solution)/shard_map/all_to_all | solution.py:160
  14.7 39.6 %copy-start.2 = (bf16[256,1024]{1,0:T(8,128)(2,1)S(1)}, bf16[256,1024]{1,0:T(8,128)(2,1)}, u32[]{:S(2)}) copy-start(bf16[256,1024]{1,0:T(8,128)(2,1)} %nodes.1) | copy-start | bytes 1572868
  14.7 37.9 %collective-permute-start.7 = (bf16[256,1024]{1,0:T(8,128)(2,1)}, bf16[256,1024]{1,0:T(8,128)(2,1)S(1)}, u32[]{:S(2)}, u32[]{:S(2)}) collective-permute-start(bf16[256,1024]{1,0:T(8,128)(2,1)} %nodes.1), channel_id=1, source_target_pairs={{0,2},{1,3},{2,4},{3,5},{4,6},{5,7},{6,8},{7,9},{8,10},{9,11},{10,... | collective-permute-start | bytes 1572872 | tf_op jit(solution)/shard_map/ppermute | solution.py:137
  17.8 35.7 %collective-permute-start.8 = (bf16[256,1024]{1,0:T(8,128)(2,1)}, bf16[256,1024]{1,0:T(8,128)(2,1)S(1)}, u32[]{:S(2)}, u32[]{:S(2)}) collective-permute-start(bf16[256,1024]{1,0:T(8,128)(2,1)} %nodes.1), channel_id=1, source_target_pairs={{0,1},{1,2},{2,3},{3,4},{4,5},{5,6},{6,7},{7,8},{8,9},{9,10},{10,1... | collective-permute-start | bytes 1572872 | tf_op jit(solution)/shard_map/ppermute | solution.py:137
  24.0 14.8 %collective-permute-start.6 = (bf16[48,1024]{1,0:T(8,128)(2,1)S(1)}, bf16[48,1024]{1,0:T(8,128)(2,1)S(1)}, u32[]{:S(2)}, u32[]{:S(2)}) collective-permute-start(bf16[48,1024]{1,0:T(8,128)(2,1)S(1)} %slice.14), channel_id=1, source_target_pairs={{0,3},{1,4},{2,5},{3,6},{4,7},{5,8},{6,9},{7,10},{8,11},{9,12},{10... | collective-permute-start | bytes 294920 | tf_op jit(solution)/shard_map/ppermute | solution.py:137
  26.3 28.8 %collective-permute-start.9 = (bf16[256,1024]{1,0:T(8,128)(2,1)}, bf16[256,1024]{1,0:T(8,128)(2,1)S(1)}, u32[]{:S(2)}, u32[]{:S(2)}) collective-permute-start(bf16[256,1024]{1,0:T(8,128)(2,1)} %nodes.1), channel_id=1, source_target_pairs={{1,0},{2,1},{3,2},{4,3},{5,4},{6,5},{7,6},{8,7},{9,8},{10,9},{11,1... | collective-permute-start | bytes 1572872 | tf_op jit(solution)/shard_map/ppermute | solution.py:137
  29.5 43.8 %collective-permute-start.10 = (bf16[256,1024]{1,0:T(8,128)(2,1)}, bf16[256,1024]{1,0:T(8,128)(2,1)}, u32[]{:S(2)}, u32[]{:S(2)}) collective-permute-start(bf16[256,1024]{1,0:T(8,128)(2,1)} %nodes.1), channel_id=1, source_target_pairs={{2,0},{3,1},{4,2},{5,3},{6,4},{7,5},{8,6},{9,7},{10,8},{11,9},{12,... | collective-permute-start | bytes 1572872 | tf_op jit(solution)/shard_map/ppermute | solution.py:137
  38.8 49.0 %collective-permute-start.11 = (bf16[80,1024]{1,0:T(8,128)(2,1)S(1)}, bf16[80,1024]{1,0:T(8,128)(2,1)S(1)}, u32[]{:S(2)}, u32[]{:S(2)}) collective-permute-start(bf16[80,1024]{1,0:T(8,128)(2,1)S(1)} %slice.15), channel_id=1, source_target_pairs={{3,0},{4,1},{5,2},{6,3},{7,4},{8,5},{9,6},{10,7},{11,8},{12,9},{13... | collective-permute-start | bytes 491528 | tf_op jit(solution)/shard_map/ppermute | solution.py:137
  56.0 1.0 copy-start.1
  63.2 33.5 %copy-start.3 = (bf16[256,512]{1,0:T(8,128)(2,1)S(1)}, bf16[256,512]{1,0:T(8,128)(2,1)}, u32[]{:S(2)}) copy-start(bf16[256,512]{1,0:T(8,128)(2,1)} %edges.1) | copy-start | bytes 786436
  63.2 33.4 %collective-permute-start.1 = (bf16[256,512]{1,0:T(8,128)(2,1)}, bf16[256,512]{1,0:T(8,128)(2,1)S(1)}, u32[]{:S(2)}, u32[]{:S(2)}) collective-permute-start(bf16[256,512]{1,0:T(8,128)(2,1)} %edges.1), channel_id=1, source_target_pairs={{0,2},{1,3},{2,4},{3,5},{4,6},{5,7},{6,8},{7,9},{8,10},{9,11},{10,... | collective-permute-start | bytes 786440 | tf_op jit(solution)/shard_map/ppermute | solution.py:137
  76.0 20.6 %collective-permute-start.2 = (bf16[256,512]{1,0:T(8,128)(2,1)}, bf16[256,512]{1,0:T(8,128)(2,1)S(1)}, u32[]{:S(2)}, u32[]{:S(2)}) collective-permute-start(bf16[256,512]{1,0:T(8,128)(2,1)} %edges.1), channel_id=1, source_target_pairs={{0,1},{1,2},{2,3},{3,4},{4,5},{5,6},{6,7},{7,8},{8,9},{9,10},{10,1... | collective-permute-start | bytes 786440 | tf_op jit(solution)/shard_map/ppermute | solution.py:137
  81.8 12.7 %collective-permute-start = (bf16[48,512]{1,0:T(8,128)(2,1)S(1)}, bf16[48,512]{1,0:T(8,128)(2,1)S(1)}, u32[]{:S(2)}, u32[]{:S(2)}) collective-permute-start(bf16[48,512]{1,0:T(8,128)(2,1)S(1)} %slice.16), channel_id=1, source_target_pairs={{0,3},{1,4},{2,5},{3,6},{4,7},{5,8},{6,9},{7,10},{8,11},{9,12},{10... | collective-permute-start | bytes 147464 | tf_op jit(solution)/shard_map/ppermute | solution.py:137
  88.5 8.3 %collective-permute-start.3 = (bf16[256,512]{1,0:T(8,128)(2,1)}, bf16[256,512]{1,0:T(8,128)(2,1)S(1)}, u32[]{:S(2)}, u32[]{:S(2)}) collective-permute-start(bf16[256,512]{1,0:T(8,128)(2,1)} %edges.1), channel_id=1, source_target_pairs={{1,0},{2,1},{3,2},{4,3},{5,4},{6,5},{7,6},{8,7},{9,8},{10,9},{11,1... | collective-permute-start | bytes 786440 | tf_op jit(solution)/shard_map/ppermute | solution.py:137
  91.7 10.3 %collective-permute-start.4 = (bf16[256,512]{1,0:T(8,128)(2,1)}, bf16[256,512]{1,0:T(8,128)(2,1)S(1)}, u32[]{:S(2)}, u32[]{:S(2)}) collective-permute-start(bf16[256,512]{1,0:T(8,128)(2,1)} %edges.1), channel_id=1, source_target_pairs={{2,0},{3,1},{4,2},{5,3},{6,4},{7,5},{8,6},{9,7},{10,8},{11,9},{12,... | collective-permute-start | bytes 786440 | tf_op jit(solution)/shard_map/ppermute | solution.py:137
  94.5 16.8 %collective-permute-start.5 = (bf16[80,512]{1,0:T(8,128)(2,1)S(1)}, bf16[80,512]{1,0:T(8,128)(2,1)S(1)}, u32[]{:S(2)}, u32[]{:S(2)}) collective-permute-start(bf16[80,512]{1,0:T(8,128)(2,1)S(1)} %slice.17), channel_id=1, source_target_pairs={{3,0},{4,1},{5,2},{6,3},{7,4},{8,5},{9,6},{10,7},{11,8},{12,9},{13... | collective-permute-start | bytes 245768 | tf_op jit(solution)/shard_map/ppermute | solution.py:137
  111.3 1.1 copy-start.4

commit v2 on v1

v2 whole, which is shorter than its diff:
```python
import functools

import jax
import jax.numpy as jnp
from jax import lax
from jax.experimental import pallas as pl
from jax.experimental.pallas import tpu as pltpu
from jax.sharding import PartitionSpec as P

HALF = 560
KEYS = 1408
OWN = 560
CHUNKS = (
    (304, 256, -1),
    (816, 256, 1),
    (48, 256, -2),
    (1072, 256, 2),
    (0, 48, -3),
    (1328, 80, 3),
)
SENDS = {
    1: (304, 0, 256),
    -1: (816, 0, 256),
    2: (48, 0, 256),
    -2: (1072, 0, 256),
    3: (0, 208, 48),
    -3: (1328, 0, 80),
}
AWAYS = tuple(SENDS)
GRID_COPIES = 4
LOG2E = 1.4426950408889634
F32 = jnp.float32
BF16 = jnp.bfloat16
MESH = pl.DeviceIdType.MESH


def dot(a, b):
    return jnp.dot(a, b, preferred_element_type=F32)


def span_of(start, size, unit):
    return pl.ds(pl.multiple_of(start, unit), size)


def encode_kernel(
    regions,
    shards,
    used,
    source,
    target,
    bias,
    gain,
    grid_hbm,
    nodes_hbm,
    row_hbm,
    node_hbm,
    edge_hbm,
    attn_hbm,
    queries,
    keys,
    values,
    state,
    bounds,
    grid,
    row_weight,
    node_weight,
    edge_weight,
    attn_weight,
    projected,
    table,
    onehot,
    picks,
    hidden,
    sums,
    nodes,
    load_sem,
    row_send,
    row_recv,
    node_send,
    node_recv,
    sum_send,
    sum_recv,
):
    rows, width = grid.shape
    tile = state.shape[0]
    blocks, edges = source.shape
    part = rows // regions
    tiles = regions * shards
    region, shard = lax.axis_index("region"), lax.axis_index("shard")
    me = region * shards + shard

    def there(away):
        return (me + away >= 0) & (me + away < tiles)

    def device(away):
        return ((me + away) // shards, lax.rem(me + away, shards))

    def peer(step):
        return lax.rem(region + step, regions)

    loads = []
    piece = rows // GRID_COPIES

    def load(source_ref, target_ref):
        copy = pltpu.make_async_copy(source_ref, target_ref, load_sem.at[len(loads)])
        copy.start()
        loads.append(copy)
        return copy

    row_load = load(row_hbm, row_weight)
    grid_loads = [
        load(grid_hbm.at[pl.ds(i * piece, piece), :], grid.at[pl.ds(i * piece, piece), :])
        for i in range(GRID_COPIES)
    ]
    node_load = load(nodes_hbm, nodes.at[pl.ds(OWN, tile), :])
    node_weight_load = load(node_hbm, node_weight)
    edge_load = load(edge_hbm, edge_weight)
    attn_load = load(attn_hbm, attn_weight)

    barrier = pltpu.get_barrier_semaphore()
    for step in range(1, regions):
        pl.semaphore_signal(barrier, inc=1, device_id=(peer(step), shard), device_id_type=MESH)
    for away in AWAYS:
        near = lax.rem(me + away + tiles, tiles)
        pl.semaphore_signal(
            barrier, inc=1, device_id=(near // shards, lax.rem(near, shards)), device_id_type=MESH
        )

    row_load.wait()
    for i in range(GRID_COPIES):
        grid_loads[i].wait()
        projected[pl.ds(i * piece, piece), :] = dot(
            grid[pl.ds(i * piece, piece), :], row_weight[...]
        ).astype(BF16)
    node_load.wait()

    pl.semaphore_wait(barrier, regions - 1 + len(AWAYS))

    here = span_of(region * part, part, part)
    row_copies = []
    for step in sorted(range(1, regions), key=lambda k: -min(k, regions - k)):
        copy = pltpu.make_async_remote_copy(
            projected.at[span_of(peer(step) * part, part, part), :],
            table.at[here, :],
            row_send.at[step - 1],
            row_recv.at[step - 1],
            device_id=(peer(step), shard),
            device_id_type=MESH,
        )
        copy.start()
        row_copies.append(copy)

    def halo(held, sends, receives, away):
        there_row, own_row, count = SENDS[away]
        slot = AWAYS.index(away)
        return pltpu.make_async_remote_copy(
            held.at[pl.ds(OWN + own_row, count), :],
            held.at[pl.ds(there_row, count), :],
            sends.at[slot],
            receives.at[slot],
            device_id=device(away),
            device_id_type=MESH,
        )

    for away in AWAYS:

        @pl.when(there(away))
        def _():
            halo(nodes, node_send, node_recv, away).start()

    table[here, :] = projected[here, :]
    node_weight_load.wait()
    table[pl.ds(rows, tile), :] = (
        dot(nodes[pl.ds(OWN, tile), :], node_weight[...]) + bias[...]
    ).astype(BF16)
    source_cols = jnp.transpose(source[...])
    target_cols = jnp.transpose(target[...])
    lane_rows = lax.broadcasted_iota(jnp.int32, (edges, rows), 1)
    lane_tile = lax.broadcasted_iota(jnp.int32, (edges, tile), 1)
    sub_tile = lax.broadcasted_iota(jnp.int32, (tile, edges), 0)
    for block in range(blocks):
        span = pl.ds(block * edges, edges)
        onehot[span, pl.ds(0, rows)] = (
            (source_cols[:, block : block + 1] == lane_rows).astype(F32).astype(BF16)
        )
        onehot[span, pl.ds(rows, tile)] = (
            (target_cols[:, block : block + 1] == lane_tile).astype(F32).astype(BF16)
        )
        goal = jnp.where(used[...] > block, target[block : block + 1, :], -1)
        picks[:, span] = (goal == sub_tile).astype(F32).astype(BF16)

    for copy in row_copies:
        copy.wait()
    step_edges = 2 * edges
    for index in range(blocks * edges // step_edges):
        span = pl.ds(index * step_edges, step_edges)
        pre = dot(onehot[span, :], table[...])
        hidden[span, :] = (0.5 * pre * (1.0 + jnp.tanh(0.5 * pre))).astype(BF16)
    sums[pl.ds(OWN, tile), :] = dot(picks[...], hidden[...]).astype(BF16)
    for away in AWAYS:

        @pl.when(there(away))
        def _():
            halo(sums, sum_send, sum_recv, away).start()

    edge_load.wait()
    attn_load.wait()

    def normalised(span):
        held = (nodes[span, :].astype(F32) + dot(sums[span, :], edge_weight[...])).astype(BF16)
        wide = held.astype(F32)
        centred = wide - jnp.mean(wide, axis=1, keepdims=True)
        spread = jnp.mean(centred * centred, axis=1, keepdims=True)
        return held, (centred * lax.rsqrt(spread + 1e-05) * gain[...]).astype(BF16)

    def project(normed, span, flag):
        key = dot(normed, attn_weight[:, width : 2 * width])
        value = dot(normed, attn_weight[:, 2 * width :]) * flag
        for pair in range(width // 128):
            lanes = slice(pair * 128, pair * 128 + 128)
            keys[pair, span, :] = key[:, lanes].astype(BF16)
            values[pair, span, :] = value[:, lanes].astype(BF16)
        return (
            jnp.max(key * key, axis=0, keepdims=True),
            jnp.max(jnp.abs(value), axis=0, keepdims=True),
        )

    held, normed = normalised(pl.ds(OWN, tile))
    state[...] = held
    query = dot(normed, attn_weight[:, :width]) * (LOG2E * 0.125)
    for pair in range(width // 128):
        queries[pair, :, :] = query[:, pair * 128 : pair * 128 + 128].astype(BF16)
    top_key, top_value = project(normed, pl.ds(OWN, tile), 1.0)
    heads = (
        lax.broadcasted_iota(jnp.int32, (width, 128), 0) // 64
        == lax.broadcasted_iota(jnp.int32, (width, 128), 1)
    )
    heads = heads.astype(F32).astype(BF16)
    query_norm = jnp.max(dot((query * query).astype(BF16), heads), axis=0, keepdims=True)

    for first, count, away in CHUNKS:
        span = pl.ds(first, count)

        @pl.when(there(away))
        def _():
            halo(nodes, node_send, node_recv, -away).wait_recv()
            halo(sums, sum_send, sum_recv, -away).wait_recv()

        @pl.when(jnp.logical_not(there(away)))
        def _():
            nodes[span, :] = nodes[pl.ds(OWN, count), :]
            sums[span, :] = sums[pl.ds(OWN, count), :]

        _, normed = normalised(span)
        new_key, new_value = project(normed, span, there(away).astype(F32))
        top_key, top_value = jnp.maximum(top_key, new_key), jnp.maximum(top_value, new_value)

    key_norm = dot(jnp.broadcast_to(top_key, (8, width)).astype(BF16), heads)
    bounds[0:8, :] = query_norm * key_norm
    bounds[8:16, :] = jnp.broadcast_to(jnp.max(top_value, axis=1, keepdims=True), (8, 128))
    for away in AWAYS:

        @pl.when(there(away))
        def _():
            halo(nodes, node_send, node_recv, away).wait_send()
            halo(sums, sum_send, sum_recv, away).wait_send()


def window_kernel(
    bounds, queries_hbm, keys_hbm, values_hbm, state, out_hbm, mixed,
    queries, keys, values, out_weight, attended, ones, sems,
):
    pairs, tile, lanes = queries.shape
    half = tile // 2
    span_keys = KEYS - half
    tiles = lax.axis_size("region") * lax.axis_size("shard")
    me = lax.axis_index("region") * lax.axis_size("shard") + lax.axis_index("shard")

    def fetch(pair):
        return [
            pltpu.make_async_copy(held.at[pair], kept.at[pair], sems.at[slot, pair])
            for slot, (held, kept) in enumerate(
                ((queries_hbm, queries), (keys_hbm, keys), (values_hbm, values))
            )
        ]

    for pair in range(pairs):
        for copy in fetch(pair):
            copy.start()
    weight_copy = pltpu.make_async_copy(out_hbm, out_weight, sems.at[3, 0])
    weight_copy.start()

    spot = lax.broadcasted_iota(jnp.int32, (KEYS, lanes), 0) - OWN + me * tile
    ones[...] = ((spot >= 0) & (spot < tiles * tile)).astype(F32).astype(BF16)
    lane = lax.broadcasted_iota(jnp.int32, (half, lanes), 1)
    row = lax.broadcasted_iota(jnp.int32, (2 * half, lanes), 0) % half
    key = lax.broadcasted_iota(jnp.int32, (2 * half, lanes), 1)
    low = key >= row
    edge = (2 * HALF) // lanes * lanes
    high = [key + at < row + 2 * HALF for at in range(edge, span_keys, lanes)]
    small = jnp.max(bounds[0:8, :]) < 6400.0
    small = small & (jnp.max(bounds[8:16, :]) < 1e9)

    def attend(pair, part, with_max):
        rows = slice(part * half, part * half + half)
        query = queries[pair, rows, :]
        zero = jnp.zeros_like(query)
        query = jnp.concatenate(
            [jnp.where(lane < 64, query, zero), jnp.where(lane >= 64, query, zero)], axis=0
        )
        near = pl.ds(part * half, span_keys)
        scores = lax.dot_general(
            query, keys[pair, near, :], (((1,), (1,)), ((), ())), preferred_element_type=F32
        )
        scores = jnp.concatenate(
            [jnp.where(low, scores[:, :lanes], -1e30), scores[:, lanes:edge]]
            + [
                jnp.where(keep, scores[:, edge + i * lanes : edge + (i + 1) * lanes], -1e30)
                for i, keep in enumerate(high)
            ],
            axis=1,
        )
        if with_max:
            scores = scores - jnp.max(scores, axis=1, keepdims=True)
            raised = jnp.exp2(scores)
            live = lax.dot_general(
                raised.astype(BF16), ones[near, :], (((1,), (0,)), ((), ())),
                preferred_element_type=F32,
            )
            weights = (raised / live[:, 0:1]).astype(BF16)
            both = dot(weights, values[pair, near, :])
        else:
            raised = jnp.exp2(scores).astype(BF16)
            both = dot(raised, jnp.concatenate([values[pair, near, :], ones[near, :]], axis=1))
            both = both[:, :lanes] / both[:, lanes:]
        attended[rows, span_of(pair * lanes, lanes, lanes)] = jnp.where(
            lane < 64, both[:half], both[half:]
        ).astype(BF16)

    def both_halves(with_max, pair, carry):
        for copy in fetch(pair):
            copy.wait()
        for part in range(2):
            attend(pair, part, with_max)
        return carry

    @pl.when(small)
    def _():
        lax.fori_loop(0, pairs, functools.partial(both_halves, False), 0, unroll=2)

    @pl.when(jnp.logical_not(small))
    def _():
        lax.fori_loop(0, pairs, functools.partial(both_halves, True), 0)

    weight_copy.wait()
    mixed[...] = (state[...].astype(F32) + dot(attended[...], out_weight[...])).astype(BF16)


VMEM = pl.BlockSpec(memory_space=pltpu.VMEM)
ANY = pl.BlockSpec(memory_space=pl.ANY)


def local(
    grid_rows,
    node_inputs,
    row_weight,
    node_weight,
    edge_bias,
    edge_out_weight,
    norm_gain,
    attn_weight,
    attn_out_weight,
    edge_source,
    edge_target,
    block_count,
):
    tile, width = node_inputs.shape
    rows = grid_rows.shape[0]
    hidden = row_weight.shape[1]
    blocks, edges = edge_source.shape
    regions, shards = lax.axis_size("region"), lax.axis_size("shard")
    pairs = width // 128
    dma = pltpu.SemaphoreType.DMA
    queries, keys, values, state, bounds = pl.pallas_call(
        functools.partial(encode_kernel, regions, shards),
        out_shape=(
            jax.ShapeDtypeStruct((pairs, tile, 128), BF16),
            jax.ShapeDtypeStruct((pairs, KEYS, 128), BF16),
            jax.ShapeDtypeStruct((pairs, KEYS, 128), BF16),
            jax.ShapeDtypeStruct((tile, width), BF16),
            jax.ShapeDtypeStruct((16, 128), F32),
        ),
        in_specs=[VMEM] * 5 + [ANY] * 6,
        out_specs=[VMEM] * 5,
        scratch_shapes=[
            pltpu.VMEM((rows, width), BF16),
            pltpu.VMEM(row_weight.shape, BF16),
            pltpu.VMEM(node_weight.shape, BF16),
            pltpu.VMEM(edge_out_weight.shape, BF16),
            pltpu.VMEM(attn_weight.shape, BF16),
            pltpu.VMEM((rows, hidden), BF16),
            pltpu.VMEM((rows + tile, hidden), BF16),
            pltpu.VMEM((blocks * edges, rows + tile), BF16),
            pltpu.VMEM((tile, blocks * edges), BF16),
            pltpu.VMEM((blocks * edges, hidden), BF16),
            pltpu.VMEM((KEYS, hidden), BF16),
            pltpu.VMEM((KEYS, width), BF16),
            dma((GRID_COPIES + 5,)),
            dma((regions - 1,)),
            dma((regions - 1,)),
            dma((len(AWAYS),)),
            dma((len(AWAYS),)),
            dma((len(AWAYS),)),
            dma((len(AWAYS),)),
        ],
        compiler_params=pltpu.CompilerParams(collective_id=0, has_side_effects=True),
        name="encode",
    )(
        jnp.broadcast_to(block_count[:, None], (1, edges)),
        edge_source,
        edge_target,
        edge_bias[None],
        norm_gain[None],
        grid_rows,
        node_inputs,
        row_weight,
        node_weight,
        edge_out_weight,
        attn_weight,
    )
    return pl.pallas_call(
        window_kernel,
        out_shape=jax.ShapeDtypeStruct((tile, width), BF16),
        in_specs=[VMEM, ANY, ANY, ANY, VMEM, ANY],
        out_specs=VMEM,
        scratch_shapes=[
            pltpu.VMEM((pairs, tile, 128), BF16),
            pltpu.VMEM((pairs, KEYS, 128), BF16),
            pltpu.VMEM((pairs, KEYS, 128), BF16),
            pltpu.VMEM((width, width), BF16),
            pltpu.VMEM((tile, width), BF16),
            pltpu.VMEM((KEYS, 128), BF16),
            dma((4, pairs)),
        ],
        name="window",
    )(bounds, queries, keys, values, state, attn_out_weight)


def solution(mesh):
    placed = (
        P(("region", "shard"), None),
        P(("region", "shard"), None),
        P(),
        P(),
        P(),
        P(),
        P(),
        P(),
        P(),
        P(("region", "shard"), None),
        P(("region", "shard"), None),
        P(("region", "shard")),
    )
    return jax.shard_map(
        local, mesh=mesh, in_specs=placed, out_specs=P(("region", "shard"), None), check_vma=False
    )
```

time: 146 us -> 99.7 us (0.68)
  the two profiles are of different devices: /device:TPU:119 before, /device:TPU:32 now
where the time goes in v2:
time: 99.7 us; the launch traced here: 99.5 us
  Pallas kernels  98.1 us (98%)
    pallas_call x1, Pallas kernels, local(): pl.pallas_call(functools.partial(encode_kernel, regions, shards), out_sha...  78.1 us
    pallas_call x1, Pallas kernels, local(): pl.pallas_call(window_kernel, out_shape=jax.ShapeDtypeStruct((tile, width...  19.9 us

profile of v2, /device:TPU:32, one launch (start us, length us, event | category | flops | bytes accessed | tf_op | source)
XLA Modules:
  0.0 99.5 jit_solution(14682074615582959977)
XLA Ops:
  0.7 0.6 broadcast_in_dim.15.used
  1.2 78.1 %encode.1 = (bf16[8,256,128]{2,1,0:T(8,128)(2,1)}, bf16[8,1408,128]{2,1,0:T(8,128)(2,1)}, bf16[8,1408,128]{2,1,0:T(8,128)(2,1)}, bf16[256,1024]{1,0:T(8,128)(2,1)}, f32[16,128]{1,0:T(8,128)}) custom-call(s32[1,128]{1,0:T(1,128)} %broadcast_in_dim.15.used, s32[16,128]{1,0:T(8,128)} %source.1, s32[16,128]{1,0:T(8,128)} %target.1, f32[1,512]{1,0:T(1,128)} %bitcast.5, ...), custom_call_target="tpu_custom_call" | custom-call | tf_op jit(solution)/shard_map/encode/pallas_call | solution.py:384
  79.4 19.9 %window.1 = bf16[256,1024]{1,0:T(8,128)(2,1)} custom-call(f32[16,128]{1,0:T(8,128)} %get-tuple-element.10.bounds, bf16[8,256,128]{2,1,0:T(8,128)(2,1)} %get-tuple-element.11.queries_hbm, bf16[8,1408,128]{2,1,0:T(8,128)(2,1)} %get-tuple-element.12.keys_hbm, bf16[8,1408,128]{2,1,0:T(8,128)(2,1)} %get-tuple-element.13.values_hbm, ...), custom_call_target="tpu_custom_call" | custom-call | tf_op jit(solution)/shard_map/window/pallas_call | solution.py:431
